TPU v7x, 32 devices: a whole 2x2x4 slice. The times are simulated.
32 devices in a mesh: slab: 8 (over z, x), snap: 4 (over y, core).
Axes of the slice: x: 2, y: 2, z: 4, core: 2. Of those that a mesh axis runs over, the one named last changes fastest.
Arguments:
- direct: bfloat16 [256, 3, 16, 1024], P('snap', None, 'slab'), may hold values from -6 to 6
- adjoint: bfloat16 [256, 3, 16, 1024], P('snap', None, 'slab'), may hold values from -6 to 6
- viscosity: float32 [16, 1024], P('slab'), may hold values from 0.3 to 3
- energy: float32 [1024], replicated, may hold values from 0.3 to 3
Outputs:
- hankel: float32 [256, 256], P(None, 'snap')
All inputs are finite; a program needn't handle non-finite values.
Results may differ from a plain program's by a relative error of at most 0.003.
Values may be sent and summed in bfloat16 or wider, within the bound.
A program may use at most 64 MiB of HBM per device.

v0:
```python
import math

import jax
import jax.numpy as jnp
from jax import lax
from jax.sharding import PartitionSpec as P

NY = 32
NZ = 32


def extended(block, sides, width):
    for axis, dim in sides:
        count = lax.axis_size(axis)
        forward = [(i, i + 1) for i in range(count - 1)]
        backward = [(target, source) for source, target in forward]
        low = lax.ppermute(
            lax.slice_in_dim(block, block.shape[dim] - width, None, axis=dim), axis, forward
        )
        high = lax.ppermute(lax.slice_in_dim(block, 0, width, axis=dim), axis, backward)
        block = jnp.concatenate([low, block, high], axis=dim)
    return block


def plane_shifts(field, ny, nz):
    cells = ny * nz
    zpos = jnp.arange(cells, dtype=jnp.int32) % nz
    blank = jnp.zeros(field.shape[:-1] + (nz,), jnp.float32)
    y_next = jnp.concatenate([field[..., nz:], blank], axis=-1)
    y_prev = jnp.concatenate([blank, field[..., :-nz]], axis=-1)
    z_next = jnp.where(
        zpos == nz - 1, jnp.roll(field, nz - 1, axis=-1), jnp.roll(field, -1, axis=-1)
    )
    z_prev = jnp.where(zpos == 0, jnp.roll(field, -(nz - 1), axis=-1), jnp.roll(field, 1, axis=-1))
    return y_next + y_prev + z_next + z_prev - 4.0 * field


def apply_operator(padded, viscosity, energy, ny, nz):
    field = padded.astype(jnp.float32)
    planes = field.shape[-2] - 4
    centre = field[..., 2 : 2 + planes, :]
    streamwise = (
        -field[..., 0:planes, :]
        + 16.0 * field[..., 1 : 1 + planes, :]
        - 30.0 * centre
        + 16.0 * field[..., 3 : 3 + planes, :]
        - field[..., 4 : 4 + planes, :]
    ) / 12.0
    lap = streamwise + plane_shifts(centre, ny, nz)
    return (energy * (viscosity * lap - centre)).astype(jnp.bfloat16)


def contract(left, right):
    return lax.dot_general(
        left, right, (((1,), (1,)), ((), ())), preferred_element_type=jnp.float32
    )


def per_device(direct, adjoint, viscosity, energy):
    local_cols = direct.shape[0]
    depth = 3 * direct.shape[2] * direct.shape[3]
    scale_factor = 1.0 / (8.0 * math.sqrt(3.0 * direct.shape[2] * lax.axis_size("slab") * NY * NZ))
    padded = extended(direct, (("slab", 2),), 2)
    weighted = apply_operator(padded, viscosity, energy, NY, NZ)
    flat_w = weighted.reshape(local_cols, depth)
    flat_a = adjoint.reshape(adjoint.shape[0], depth)
    partial_tiles = contract(lax.all_gather(flat_a, "snap", axis=0, tiled=True), flat_w)
    summed = lax.psum(partial_tiles, "slab")
    return summed * scale_factor


def solution(mesh):
    placed = (P("snap", None, "slab", None), P("snap", None, "slab", None), P("slab", None), P())
    return jax.shard_map(
        per_device, mesh=mesh, in_specs=placed, out_specs=P(None, "snap"), check_vma=False
    )
```

profile of v0, /device:TPU:0, one launch (start us, length us, event | category | flops | bytes accessed | tf_op | source)
XLA Modules:
  0.0 153.4 jit_solution(2399825513757516703)
XLA Ops:
  6.5 0.0 copy-start
  6.5 0.0 all-gather.2.cloned.1.call-start
  6.5 1.4 collective-permute-start.1
  8.0 5.5 %collective-permute-start = (bf16[64,3,2,1024]{3,2,1,0:T(2,128)(2,1)}, bf16[64,3,2,1024]{3,2,1,0:T(2,128)(2,1)S(1)}, u32[]{:S(2)}, u32[]{:S(2)}) collective-permute-start(bf16[64,3,2,1024]{3,2,1,0:T(2,128)(2,1)} %param.4), channel_id=1, source_target_pairs={{0,4},{4,8},{8,12},{12,16},{16,20},{20,24},{24,28},{1,5},{5,9},{9,... | collective-permute-start | bytes 2359304 | tf_op jit(solution)/shard_map/ppermute | solution.py:17
  13.5 3.3 %reshape.9 = bf16[64,6144]{1,0:T(8,128)(2,1)} reshape(bf16[64,3,2,1024]{3,2,1,0:T(2,128)(2,1)} %param.5) | data formatting | bytes 1572864 | tf_op jit(solution)/shard_map/reshape | solution.py:66
  16.8 0.0 all-gather.2.cloned.1.call-update
  16.8 0.0 all-reduce.4.cloned.1.call-start
  16.9 12.4 %collective-permute-done.1 = bf16[64,3,2,1024]{3,2,1,0:T(2,128)(2,1)S(1)} collective-permute-done((bf16[64,3,2,1024]{3,2,1,0:T(2,128)(2,1)}, bf16[64,3,2,1024]{3,2,1,0:T(2,128)(2,1)S(1)}, u32[]{:S(2)}, u32[]{:S(2)}) %collective-permute-start.1) | collective-permute-done | bytes 786464 | tf_op jit(solution)/shard_map/ppermute | solution.py:20
  29.3 17.1 %collective-permute-done = bf16[64,3,2,1024]{3,2,1,0:T(2,128)(2,1)S(1)} collective-permute-done((bf16[64,3,2,1024]{3,2,1,0:T(2,128)(2,1)}, bf16[64,3,2,1024]{3,2,1,0:T(2,128)(2,1)S(1)}, u32[]{:S(2)}, u32[]{:S(2)}) %collective-permute-start) | collective-permute-done | bytes 786464 | tf_op jit(solution)/shard_map/ppermute | solution.py:17
  46.4 0.0 copy-done
  46.4 0.8 maximum_convert_fusion.3
  47.2 0.8 maximum_convert_fusion.4
  48.0 2.7 %maximum_convert_fusion = f32[64,3,6,1024]{3,2,1,0:T(8,128)S(1)} fusion(bf16[64,3,2,1024]{3,2,1,0:T(2,128)(2,1)S(1)} %collective-permute-done.1, bf16[64,3,2,1024]{3,2,1,0:T(2,128)(2,1)S(1)} %copy-done, bf16[64,3,2,1024]{3,2,1,0:T(2,128)(2,1)S(1)} %collective-permute-done), kind=kLoop, calls=%fused_computation | loop fusion | flops 7077888 | bytes 7077888 | tf_op jit(solution)/shard_map/convert_element_type | solution.py:39
  50.7 3.2 %fusion.17 = (f32[64,3,2,1023]{3,2,1,0:T(2,128)S(1)}, f32[64,3,2,1023]{3,2,1,0:T(2,128)S(1)}) fusion(f32[64,3,6,1024]{3,2,1,0:T(8,128)S(1)} %maximum_convert_fusion), kind=kLoop, calls=%fused_computation.33 | loop fusion | bytes 6285312 | tf_op jit(solution)/shard_map/jit(_roll_static)/slice | solution.py:32
  53.9 3.2 %fusion.16 = (f32[64,3,2,993]{3,2,1,0:T(2,128)S(1)}, f32[64,3,2,993]{3,2,1,0:T(2,128)S(1)}) fusion(f32[64,3,6,1024]{3,2,1,0:T(8,128)S(1)} %maximum_convert_fusion), kind=kLoop, calls=%fused_computation.32 | loop fusion | bytes 6100992 | tf_op jit(solution)/shard_map/jit(_roll_static)/slice | solution.py:32
  57.1 0.0 copy-start.1
  57.1 0.0 copy-start.2
  57.1 3.2 %fusion.15 = (f32[64,3,2,992]{3,2,1,0:T(2,128)S(1)}, f32[64,3,2,992]{3,2,1,0:T(2,128)S(1)}) fusion(f32[64,3,6,1024]{3,2,1,0:T(8,128)S(1)} %maximum_convert_fusion), kind=kLoop, calls=%fused_computation.31 | loop fusion | bytes 6094848 | tf_op jit(solution)/shard_map/slice | solution.py:29
  60.4 0.0 copy-done.1
  60.4 0.0 copy-done.2
  60.4 9.9 %multiply_convert_fusion = bf16[64,3,2,1024]{3,2,1,0:T(2,128)(2,1)S(1)} fusion(f32[64,3,2,1023]{3,2,1,0:T(2,128)S(1)} %get-tuple-element.10, f32[64,3,2,1]{3,2,1,0:T(2,128)S(1)} %get-tuple-element.14, f32[64,3,2,31]{3,2,1,0:T(2,128)S(1)} %get-tuple-element.12, f32[64,3,2,993]{3,2,1,0:T(2,128)S(1)} %get-tuple-element.8, ...), kind=kLoop, calls=%fused_computation.17 | loop fusion | flops 9830400 | bytes 18003968 | tf_op jit(solution)/shard_map/convert_element_type | solution.py:50
  70.3 0.6 reshape.8
  70.9 0.0 all-gather.2.cloned.1.call-done
  70.9 3.6 %convolution_bitcast_fusion = f32[256,64]{0,1:T(8,128)} fusion(bf16[64,6144]{1,0:T(8,128)(2,1)S(1)} %reshape.8, bf16[256,6144]{1,0:T(8,128)(2,1)} %all-gather.2.cloned.1.call-done), kind=kOutput, calls=%fused_computation.18 | convolution fusion | flops 201326592 | bytes 3997696 | tf_op jit(solution)/shard_map/dot_general | solution.py:54
  74.5 0.0 all-reduce.4.cloned.1.call-update
  74.5 70.5 %all-reduce.4.cloned.1.call-done = f32[256,64]{0,1:T(8,128)} async-done(((f32[256,64]{0,1:T(8,128)}), f32[256,64]{0,1:T(8,128)}) %all-reduce.4.cloned.1.call-update) | async-done | bytes 65552 | tf_op jit(solution)/shard_map/psum | solution.py:68
  145.1 1.5 broadcast_multiply_fusion
  (1 shorter events, 0.0 us)
Async XLA Ops:
  6.5 39.9 %copy-start = (bf16[64,3,2,1024]{3,2,1,0:T(2,128)(2,1)S(1)}, bf16[64,3,2,1024]{3,2,1,0:T(2,128)(2,1)}, u32[]{:S(2)}) copy-start(bf16[64,3,2,1024]{3,2,1,0:T(2,128)(2,1)} %param.4) | copy-start | bytes 2359300
  6.5 64.4 %all-gather.2.cloned.1.call-start = ((), (), s32[]{:S(2)}) async-start(), calls=%async_computation | async-start | bytes 3932160 | tf_op jit(solution)/shard_map/all_gather | solution.py:67
  6.5 22.7 %collective-permute-start.1 = (bf16[64,3,2,1024]{3,2,1,0:T(2,128)(2,1)}, bf16[64,3,2,1024]{3,2,1,0:T(2,128)(2,1)S(1)}, u32[]{:S(2)}, u32[]{:S(2)}) collective-permute-start(bf16[64,3,2,1024]{3,2,1,0:T(2,128)(2,1)} %param.4), channel_id=1, source_target_pairs={{4,0},{8,4},{12,8},{16,12},{20,16},{24,20},{28,24},{5,1},{9,5},{13... | collective-permute-start | bytes 2359304 | tf_op jit(solution)/shard_map/ppermute | solution.py:20
  8.0 38.4 %collective-permute-start = (bf16[64,3,2,1024]{3,2,1,0:T(2,128)(2,1)}, bf16[64,3,2,1024]{3,2,1,0:T(2,128)(2,1)S(1)}, u32[]{:S(2)}, u32[]{:S(2)}) collective-permute-start(bf16[64,3,2,1024]{3,2,1,0:T(2,128)(2,1)} %param.4), channel_id=1, source_target_pairs={{0,4},{4,8},{8,12},{12,16},{16,20},{20,24},{24,28},{1,5},{5,9},{9,... | collective-permute-start | bytes 2359304 | tf_op jit(solution)/shard_map/ppermute | solution.py:17
  16.8 128.3 %all-reduce.4.cloned.1.call-start = ((), (), s32[]{:S(2)}) async-start(), calls=%async_computation.1 | async-start | bytes 131072 | tf_op jit(solution)/shard_map/psum | solution.py:68
  57.1 3.2 %copy-start.1 = (f32[2,1024]{1,0:T(2,128)S(1)}, f32[2,1024]{1,0:T(2,128)}, u32[]{:S(2)}) copy-start(f32[2,1024]{1,0:T(2,128)} %param.6) | copy-start | bytes 24580
  57.1 3.2 %copy-start.2 = (f32[1024]{0:T(1024)S(1)}, f32[1024]{0:T(1024)}, u32[]{:S(2)}) copy-start(f32[1024]{0:T(1024)} %param.7) | copy-start | bytes 12292
Sparse Core Ops, SparseCore 0:
  16.9 30.1 all-gather.1
  74.6 70.3 all-reduce.3
where the time goes:
time: 154 us; the launch traced here: 153 us
  waiting for transfers between devices  100 us (65%)
  other arithmetic  15.6 us (10%)
  local copies, waits for them, and re-layouts  13.5 us (9%)
  between operations  13.5 us (9%)
  starting transfers between devices  7 us (5%)
  matrix products  3.6 us (2%)
    psum x1, waiting for transfers between devices, per_device(): summed = lax.psum(partial_tiles, 'slab')  70.5 us
    ppermute x1, waiting for transfers between devices, extended(): lax.ppermute(lax.slice_in_dim(block, block.shape[dim] - width, None, axis...  17.1 us
    ppermute x1, waiting for transfers between devices, extended(): lax.ppermute(lax.slice_in_dim(block, 0, width, axis=dim), axis, backward)  12.4 us
    convert_element_type x1, other arithmetic, apply_operator(): return (energy * (viscosity * lap - centre)).astype(jnp.bfloat16)  9.88 us
    ppermute x1, starting transfers between devices, extended(): lax.ppermute(lax.slice_in_dim(block, block.shape[dim] - width, None, axis...  5.55 us
    dot_general x1, matrix products, contract(): lax.dot_general(left, right, (((1,), (1,)), ((), ())), preferred_element_...  3.6 us
    reshape x1, local copies, waits for them, and re-layouts, per_device(): flat_a = adjoint.reshape(adjoint.shape[0], depth)  3.25 us
    slice x1, local copies, waits for them, and re-layouts, plane_shifts(): y_next = jnp.concatenate([field[..., nz:], blank], axis=-1)  3.21 us
  transfers between devices with their start and end apart: 4, of which 3 were waited for; matrix products, arithmetic and copies ran while one was open for 18% of the time, Pallas kernels for 0%

commit v1 on v0

v1 whole, which is shorter than its diff:
```python
import functools
import math

import jax
import jax.numpy as jnp
import numpy as np
from jax import lax
from jax.experimental import pallas as pl
from jax.experimental.pallas import tpu as pltpu
from jax.sharding import PartitionSpec as P

NY = 32
NZ = 32
LANES = 128
QUARTERS = 4
HALVES = 2
LAG = 2


def plane_matrix():
    inner = np.zeros((LANES, LANES), np.float32)
    up = np.zeros((LANES, LANES), np.float32)
    down = np.zeros((LANES, LANES), np.float32)
    for lane in range(LANES):
        row, z = divmod(lane, NZ)
        inner[lane, lane] -= 4.0
        inner[row * NZ + (z + 1) % NZ, lane] += 1.0
        inner[row * NZ + (z - 1) % NZ, lane] += 1.0
        if lane + NZ < LANES:
            inner[lane + NZ, lane] += 1.0
        else:
            down[lane + NZ - LANES, lane] += 1.0
        if lane - NZ >= 0:
            inner[lane - NZ, lane] += 1.0
        else:
            up[lane - NZ + LANES, lane] += 1.0
    return np.concatenate([inner, up, down], axis=1)


def kernel(slabs, snaps, reduce_here, scale,
           d_ref, a_ref, v_ref, e_ref, m_ref, out_ref,
           dv, halo, av, at, wt, ab, wb, e16, acc, rs,
           loc_sem, px_s, px_r, pz_s, pz_r, ac_s, ac_r, ay_s, ay_r, af_s, af_r,
           rs_s, rs_r, ag_s, ag_r):
    cols, comps, rows = d_ref.shape[0], d_ref.shape[1], d_ref.shape[2]
    chips = snaps // 2
    i = lax.axis_index("slab")
    n = lax.axis_index("snap")
    parity = i % 2
    pair = i + 1 - 2 * parity
    step = 2 - 4 * parity
    z_to = i + step
    z_from = i - step
    has_to = jnp.logical_and(z_to >= 0, z_to < slabs)
    has_from = jnp.logical_and(z_from >= 0, z_from < slabs)
    chip, core = n // 2, n % 2
    mate = chip * 2 + 1 - core
    pair_slot = 1 - parity
    z_slot = parity
    dq = cols // QUARTERS
    ah = cols // HALVES

    def dev(slab, snap):
        return {"slab": slab, "snap": snap}

    barrier = pltpu.get_barrier_semaphore()

    def greet(slab, snap):
        pl.semaphore_signal(barrier, 1, device_id=dev(slab, snap),
                            device_id_type=pl.DeviceIdType.MESH)

    greet(i, mate)
    for t in range(1, chips):
        greet(i, ((chip + t) % chips) * 2 + core)
    if reduce_here:
        for k in range(1, slabs):
            greet((i + k) % slabs, n)
        pl.semaphore_wait(barrier, chips + slabs - 1)
    else:
        greet(pair, n)

        @pl.when(has_to)
        def _():
            greet(z_to, n)

        @pl.when(has_from)
        def _():
            greet(z_from, n)

        pl.semaphore_wait(
            barrier, chips + 1 + has_to.astype(jnp.int32) + has_from.astype(jnp.int32))

    def remote(src, dst, s, r, slab, snap):
        return pltpu.make_async_remote_copy(
            src_ref=src, dst_ref=dst, send_sem=s, recv_sem=r,
            device_id=dev(slab, snap), device_id_type=pl.DeviceIdType.MESH)

    def px(c, q):
        part = pl.ds(q * dq, dq)
        return remote(d_ref.at[part, c], halo.at[parity, part, c],
                      px_s.at[c, q], px_r.at[c, q], pair, n)

    def pz(c, q):
        part = pl.ds(q * dq, dq)
        return remote(halo.at[pair_slot, part, c], halo.at[z_slot, part, c],
                      pz_s.at[c, q], pz_r.at[c, q], z_to, n)

    def ac(c):
        return remote(a_ref.at[:, c], av.at[n, :, c], ac_s.at[c], ac_r.at[c], i, mate)

    def ay(t, c, h):
        part = pl.ds(h * ah, ah)
        return remote(a_ref.at[part, c], av.at[n, part, c],
                      ay_s.at[t, c, h], ay_r.at[t, c, h], i, ((chip + t) % chips) * 2 + core)

    def af(t, c, h):
        part = pl.ds(h * ah, ah)
        source = ((chip + chips - t) % chips) * 2 + core
        return remote(av.at[source, part, c], av.at[source, part, c],
                      af_s.at[t, c, h], af_r.at[t, c, h], i, mate)

    def local_d(c):
        return pltpu.make_async_copy(d_ref.at[:, c], dv.at[:, c], loc_sem.at[0, c])

    def local_a(c):
        return pltpu.make_async_copy(a_ref.at[:, c], av.at[n, :, c], loc_sem.at[1, c])

    for c in range(comps):
        for q in range(QUARTERS):
            px(c, q).start()
        for h in range(HALVES):
            for t in range(1, chips):
                ay(t, c, h).start()
    for c in range(comps):
        local_d(c).start()
        local_a(c).start()
        ac(c).start()

    for j in range(rows // 2):
        e16[2 * j:2 * j + 2, :] = jnp.broadcast_to(e_ref[j:j + 1, :], (2, LANES))

    @pl.when(jnp.logical_not(has_from))
    def _():
        halo[z_slot] = jnp.zeros(halo.shape[1:], halo.dtype)

    group = 4
    span = group * rows
    row_at = lax.broadcasted_iota(jnp.int32, (span, LANES), 0)
    odd = row_at % 2 == 1
    in_snap = row_at % rows

    def stencil(c, q):
        v = jnp.concatenate([v_ref[...]] * group, axis=0)
        e = jnp.concatenate([e16[...]] * group, axis=0)

        def body(g, carry):
            at_snap = q * dq + g * group
            part = pl.ds(at_snap, group)
            o16 = dv[part, c].reshape(span, LANES)
            lo = halo[0, part, c].reshape(span, LANES).astype(jnp.float32)
            hi = halo[1, part, c].reshape(span, LANES).astype(jnp.float32)
            o = o16.astype(jnp.float32)
            y = jnp.dot(o16, m_ref[...], preferred_element_type=jnp.float32)
            t = o + jnp.where(odd, lo, hi)
            swapped = jnp.where(odd, pltpu.roll(t, 1, 0), pltpu.roll(t, span - 1, 0))
            stream = (16.0 * swapped - 30.0 * o - lo - hi) * (1.0 / 12.0)
            up = pltpu.roll(y[:, LANES:2 * LANES], 2, 0)
            down = pltpu.roll(y[:, 2 * LANES:], span - 2, 0)
            lap = stream + y[:, :LANES]
            lap = lap + jnp.where(in_snap >= 2, up, 0.0)
            lap = lap + jnp.where(in_snap < rows - 2, down, 0.0)
            wt[pl.ds(pl.multiple_of(at_snap * rows, span), span), :] = e * (v * lap - o)
            return carry

        lax.fori_loop(0, dq // group, body, 0)

    def multiply(c):
        def widen(b, carry):
            at[pl.ds(pl.multiple_of(b * cols * rows, cols * rows), cols * rows), :] = (
                av[b, :, c].reshape(cols * rows, LANES).astype(jnp.float32))
            return carry

        lax.fori_loop(0, snaps, widen, 0)
        for r in range(rows):
            ab[:, r * LANES:(r + 1) * LANES] = at[
                pl.ds(r, snaps * cols, stride=rows), :].astype(jnp.bfloat16)
            wb[:, r * LANES:(r + 1) * LANES] = wt[
                pl.ds(r, cols, stride=rows), :].astype(jnp.bfloat16)
        tile = lax.dot_general(wb[...], ab[...], (((1,), (1,)), ((), ())),
                               preferred_element_type=jnp.float32)
        if c == 0:
            acc[...] = tile
        else:
            acc[...] += tile

    def finish(g):
        c, q = divmod(g, QUARTERS)
        if q == 0:
            local_d(c).wait()

        @pl.when(has_from)
        def _():
            pz(c, q).wait_recv()

        stencil(c, q)
        if q == QUARTERS - 1:
            local_a(c).wait()
            ac(c).wait_recv()
            for t in range(1, chips):
                for h in range(HALVES):
                    af(t, c, h).wait_recv()
            multiply(c)

    total = comps * QUARTERS
    per_half = QUARTERS // HALVES
    for g in range(total):
        c, q = divmod(g, QUARTERS)
        px(c, q).wait_recv()

        @pl.when(has_to)
        def _():
            pz(c, q).start()

        if q % per_half == per_half - 1:
            h = q // per_half
            for t in range(1, chips):
                ay(t, c, h).wait_recv()
                af(t, c, h).start()
        if g >= LAG:
            finish(g - LAG)
    for g in range(total - LAG, total):
        finish(g)

    if reduce_here:
        share = cols // slabs

        def rows_of(slab):
            return pl.ds(pl.multiple_of(slab * share, share), share)

        def scatter(k):
            to = (i + k) % slabs
            return remote(acc.at[rows_of(to)], rs.at[k], rs_s.at[k], rs_r.at[k], to, n)

        def gather(k):
            return remote(rs.at[0], out_ref.at[rows_of(i)], ag_s.at[k], ag_r.at[k],
                          (i + k) % slabs, n)

        def gathered(k):
            source = (i + slabs - k) % slabs
            return remote(rs.at[0], out_ref.at[rows_of(source)], ag_s.at[k], ag_r.at[k],
                          (i + k) % slabs, n)

        for k in range(1, slabs):
            scatter(k).start()
        summed = acc[rows_of(i), :]
        for k in range(1, slabs):
            scatter(k).wait_recv()
            summed = summed + rs[k]
        summed = summed * scale
        rs[0] = summed
        for k in range(1, slabs):
            gather(k).start()
        out_ref[rows_of(i), :] = summed
        for k in range(1, slabs):
            gathered(k).wait_recv()
        for k in range(1, slabs):
            scatter(k).wait_send()
            gather(k).wait_send()
    else:
        out_ref[...] = acc[...] * scale

    for c in range(comps):
        ac(c).wait_send()
        for q in range(QUARTERS):
            px(c, q).wait_send()

            @pl.when(has_to)
            def _():
                pz(c, q).wait_send()

        for t in range(1, chips):
            for h in range(HALVES):
                ay(t, c, h).wait_send()
                af(t, c, h).wait_send()


def tiles_first(block):
    lead, (planes, cells) = block.shape[:-2], block.shape[-2:]
    split = block.reshape(lead + (planes, cells // LANES, LANES))
    return jnp.swapaxes(split, -3, -2).reshape(lead + (planes * cells // LANES, LANES))


def per_device(slabs, snaps, direct, adjoint, viscosity, energy):
    cols, comps, planes, cells = direct.shape
    rows = planes * cells // LANES
    scale = 1.0 / (8.0 * math.sqrt(comps * planes * slabs * cells))
    reduce_here = cols % (8 * slabs) == 0
    share = cols // slabs if reduce_here else 8
    halves = (snaps // 2, comps, HALVES)
    quarters = (comps, QUARTERS)
    dma = pltpu.SemaphoreType.DMA
    block = (cols, comps, rows, LANES)
    vmem = pl.BlockSpec(memory_space=pltpu.VMEM)
    hbm = pl.BlockSpec(memory_space=pltpu.HBM)
    out = pl.pallas_call(
        functools.partial(kernel, slabs, snaps, reduce_here, scale),
        out_shape=jax.ShapeDtypeStruct((cols, snaps * cols), jnp.float32),
        in_specs=[hbm, hbm, vmem, vmem, vmem],
        out_specs=vmem,
        scratch_shapes=[
            pltpu.VMEM(block, jnp.bfloat16),
            pltpu.VMEM((2,) + block, jnp.bfloat16),
            pltpu.VMEM((snaps,) + block, jnp.bfloat16),
            pltpu.VMEM((snaps * cols * rows, LANES), jnp.float32),
            pltpu.VMEM((cols * rows, LANES), jnp.float32),
            pltpu.VMEM((snaps * cols, rows * LANES), jnp.bfloat16),
            pltpu.VMEM((cols, rows * LANES), jnp.bfloat16),
            pltpu.VMEM((rows, LANES), jnp.float32),
            pltpu.VMEM((cols, snaps * cols), jnp.float32),
            pltpu.VMEM((max(slabs, 1) if reduce_here else 1, share, snaps * cols), jnp.float32),
            dma((2, comps)),
            dma(quarters), dma(quarters),
            dma(quarters), dma(quarters),
            dma((comps,)), dma((comps,)),
            dma(halves), dma(halves),
            dma(halves), dma(halves),
            dma((slabs,)), dma((slabs,)),
            dma((slabs,)), dma((slabs,)),
        ],
        compiler_params=pltpu.CompilerParams(collective_id=0, has_side_effects=True),
    )(
        tiles_first(direct), tiles_first(adjoint), tiles_first(viscosity),
        energy.reshape(cells // LANES, LANES), jnp.asarray(plane_matrix(), jnp.bfloat16),
    )
    if not reduce_here:
        out = lax.psum(out, "slab")
    return out.T


def solution(mesh):
    placed = (P("snap", None, "slab", None), P("snap", None, "slab", None), P("slab", None), P())
    body = functools.partial(per_device, mesh.shape["slab"], mesh.shape["snap"])
    return jax.shard_map(
        body, mesh=mesh, in_specs=placed, out_specs=P(None, "snap"), check_vma=False
    )
```

time: 154 us -> 44.5 us (0.29)
  waiting for transfers between devices: 100 us -> 0 us
  Pallas kernels: 0 us -> 42.8 us
  other arithmetic: 15.6 us -> 0 us
  between operations: 13.5 us -> 0.01 us
  local copies, waits for them, and re-layouts: 13.5 us -> 1.47 us
  starting transfers between devices: 7 us -> 0 us
  matrix products: 3.6 us -> 0 us
    psum x1 -> x0, waiting for transfers between devices: 70.5 us -> none  [per_device(): summed = lax.psum(partial_tiles, 'slab')]
    pallas_call x0 -> x1, Pallas kernels: none -> 42.8 us  [per_device(): pl.pallas_call(functools.partial(kernel, slabs, snaps, reduce_here, scale...]
    ppermute x2 -> x0, waiting for transfers between devices: 29.5 us -> none  [the longest x1 17.1 us: extended(): lax.ppermute(lax.slice_in_dim(block, block.shape[dim] - width, None, axis...]
    convert_element_type x2 -> x0, other arithmetic: 12.5 us -> none  [the longest x1 9.88 us: apply_operator(): return (energy * (viscosity * lap - centre)).astype(jnp.bfloat16)]
    slice x3 -> x0, local copies, waits for them, and re-layouts: 9.63 us -> none  [the longest x1 3.21 us: plane_shifts(): y_next = jnp.concatenate([field[..., nz:], blank], axis=-1)]
    ppermute x2 -> x0, starting transfers between devices: 6.96 us -> none  [the longest x1 5.55 us: extended(): lax.ppermute(lax.slice_in_dim(block, block.shape[dim] - width, None, axis...]
    reshape x2 -> x0, local copies, waits for them, and re-layouts: 3.85 us -> none  [the longest x1 3.25 us: per_device(): flat_a = adjoint.reshape(adjoint.shape[0], depth)]
    dot_general x1 -> x0, matrix products: 3.6 us -> none  [contract(): lax.dot_general(left, right, (((1,), (1,)), ((), ())), preferred_element_...]
  transfers between devices with their start and end apart: 4 -> 0, of which waited for: 3 -> 0; matrix products, arithmetic and copies ran while one was open for 18% -> 0% of each run, Pallas kernels for 0% -> 0%
where the time goes in v1:
time: 44.5 us; the launch traced here: 44.3 us
  Pallas kernels  42.8 us (96%)
  local copies, waits for them, and re-layouts  1.47 us (3%)
    pallas_call x1, Pallas kernels, per_device(): pl.pallas_call(functools.partial(kernel, slabs, snaps, reduce_here, scale...  42.8 us
    unnamed x1, local copies, waits for them, and re-layouts  1.47 us

profile of v1, /device:TPU:0, one launch (start us, length us, event | category | flops | bytes accessed | tf_op | source)
XLA Modules:
  0.0 44.3 jit_solution(13578090891693312145)
XLA Ops:
  0.0 42.8 %shard_map.55 = f32[64,256]{1,0:T(8,128)} custom-call(bf16[64,3,16,128]{3,2,1,0:T(8,128)(2,1)} %bitcast.17, bf16[64,3,16,128]{3,2,1,0:T(8,128)(2,1)} %bitcast.18, f32[16,128]{1,0:T(8,128)} %bitcast.20, f32[8,128]{1,0:T(8,128)} %bitcast.21, bf16[128,384]{1,0:T(8,128)(2,1)} %constant.2.clone.m_ref), custom_call_target="tpu_custom_call" | custom-call | tf_op jit(solution)/shard_map/pallas_call | solution.py:305
  42.9 1.5 %copy.10 = f32[256,64]{0,1:T(8,128)} copy(f32[256,64]{0,1:T(8,128)} %bitcast.19) | data formatting | bytes 131072

commit v2 on v1

--- a/solution.py
+++ b/solution.py
@@ -15,6 +15,7 @@
 QUARTERS = 4
 HALVES = 2
 LAG = 2
+GROUP = 16
 
 
 def plane_matrix():
@@ -38,8 +39,8 @@
 
 
 def kernel(slabs, snaps, reduce_here, scale,
-           d_ref, a_ref, v_ref, e_ref, m_ref, out_ref,
-           dv, halo, av, at, wt, ab, wb, e16, acc, rs,
+           d_ref, a_ref, v_hbm, e_hbm, m_hbm, out_ref,
+           v_ref, e_ref, m_ref, far, dv, halo, av, at, wt, ab, wb, e16, acc, rs,
            loc_sem, px_s, px_r, pz_s, pz_r, ac_s, ac_r, ay_s, ay_r, af_s, af_r,
            rs_s, rs_r, ag_s, ag_r):
     cols, comps, rows = d_ref.shape[0], d_ref.shape[1], d_ref.shape[2]
@@ -58,37 +59,11 @@
     pair_slot = 1 - parity
     z_slot = parity
     dq = cols // QUARTERS
+    per_half = QUARTERS // HALVES
     ah = cols // HALVES
 
     def dev(slab, snap):
         return {"slab": slab, "snap": snap}
-
-    barrier = pltpu.get_barrier_semaphore()
-
-    def greet(slab, snap):
-        pl.semaphore_signal(barrier, 1, device_id=dev(slab, snap),
-                            device_id_type=pl.DeviceIdType.MESH)
-
-    greet(i, mate)
-    for t in range(1, chips):
-        greet(i, ((chip + t) % chips) * 2 + core)
-    if reduce_here:
-        for k in range(1, slabs):
-            greet((i + k) % slabs, n)
-        pl.semaphore_wait(barrier, chips + slabs - 1)
-    else:
-        greet(pair, n)
-
-        @pl.when(has_to)
-        def _():
-            greet(z_to, n)
-
-        @pl.when(has_from)
-        def _():
-            greet(z_from, n)
-
-        pl.semaphore_wait(
-            barrier, chips + 1 + has_to.astype(jnp.int32) + has_from.astype(jnp.int32))
 
     def remote(src, dst, s, r, slab, snap):
         return pltpu.make_async_remote_copy(
@@ -124,6 +99,37 @@
 
     def local_a(c):
         return pltpu.make_async_copy(a_ref.at[:, c], av.at[n, :, c], loc_sem.at[1, c])
+
+    barrier = pltpu.get_barrier_semaphore()
+
+    def greet(slab, snap):
+        pl.semaphore_signal(barrier, 1, device_id=dev(slab, snap),
+                            device_id_type=pl.DeviceIdType.MESH)
+
+    greet(i, mate)
+    for t in range(1, chips):
+        greet(i, ((chip + t) % chips) * 2 + core)
+    near = 1 + has_to.astype(jnp.int32) + has_from.astype(jnp.int32)
+
+    def tell_near(sem):
+        def tell(slab):
+            pl.semaphore_signal(sem, 1, device_id=dev(slab, n),
+                                device_id_type=pl.DeviceIdType.MESH)
+
+        tell(pair)
+        pl.when(has_to)(lambda: tell(z_to))
+        pl.when(has_from)(lambda: tell(z_from))
+
+    tell_near(barrier)
+    small = [pltpu.make_async_copy(v_hbm, v_ref, loc_sem.at[2, 0]),
+             pltpu.make_async_copy(e_hbm, e_ref, loc_sem.at[2, 1]),
+             pltpu.make_async_copy(m_hbm, m_ref, loc_sem.at[2, 2])]
+    for copy in small:
+        copy.start()
+    for c in range(comps):
+        local_d(c).start()
+        local_a(c).start()
+    pl.semaphore_wait(barrier, chips + near)
 
     for c in range(comps):
         for q in range(QUARTERS):
@@ -132,10 +138,9 @@
             for t in range(1, chips):
                 ay(t, c, h).start()
     for c in range(comps):
-        local_d(c).start()
-        local_a(c).start()
         ac(c).start()
-
+    for copy in small:
+        copy.wait()
     for j in range(rows // 2):
         e16[2 * j:2 * j + 2, :] = jnp.broadcast_to(e_ref[j:j + 1, :], (2, LANES))
 
@@ -143,7 +148,7 @@
     def _():
         halo[z_slot] = jnp.zeros(halo.shape[1:], halo.dtype)
 
-    group = 4
+    group = GROUP
     span = group * rows
     row_at = lax.broadcasted_iota(jnp.int32, (span, LANES), 0)
     odd = row_at % 2 == 1
@@ -174,16 +179,19 @@
 
         lax.fori_loop(0, dq // group, body, 0)
 
+    def widen(b, c, h):
+        first = b * cols + h * ah
+        at[...] = av[b, pl.ds(h * ah, ah), c].reshape(ah * rows, LANES).astype(jnp.float32)
+        for r in range(rows):
+            ab[pl.ds(pl.multiple_of(first, ah), ah), r * LANES:(r + 1) * LANES] = at[
+                pl.ds(r, ah, stride=rows), :].astype(jnp.bfloat16)
+
+    def widen_chip(chip_at, c, h):
+        for b in range(2):
+            widen(chip_at * 2 + b, c, h)
+
     def multiply(c):
-        def widen(b, carry):
-            at[pl.ds(pl.multiple_of(b * cols * rows, cols * rows), cols * rows), :] = (
-                av[b, :, c].reshape(cols * rows, LANES).astype(jnp.float32))
-            return carry
-
-        lax.fori_loop(0, snaps, widen, 0)
         for r in range(rows):
-            ab[:, r * LANES:(r + 1) * LANES] = at[
-                pl.ds(r, snaps * cols, stride=rows), :].astype(jnp.bfloat16)
             wb[:, r * LANES:(r + 1) * LANES] = wt[
                 pl.ds(r, cols, stride=rows), :].astype(jnp.bfloat16)
         tile = lax.dot_general(wb[...], ab[...], (((1,), (1,)), ((), ())),
@@ -197,25 +205,33 @@
         c, q = divmod(g, QUARTERS)
         if q == 0:
             local_d(c).wait()
+        if q % per_half == per_half - 1:
+            h = q // per_half
+            for t in range(1, chips):
+                af(t, c, h).wait_recv()
+                widen_chip((chip + chips - t) % chips, c, h)
 
         @pl.when(has_from)
         def _():
             pz(c, q).wait_recv()
 
         stencil(c, q)
-        if q == QUARTERS - 1:
+        if q == 0:
             local_a(c).wait()
             ac(c).wait_recv()
-            for t in range(1, chips):
-                for h in range(HALVES):
-                    af(t, c, h).wait_recv()
+            for h in range(HALVES):
+                widen_chip(chip, c, h)
+        if q == QUARTERS - 1:
             multiply(c)
 
     total = comps * QUARTERS
-    per_half = QUARTERS // HALVES
+    rounds = slabs // 2 - 1 if reduce_here else 0
+    assert rounds <= total
     for g in range(total):
         c, q = divmod(g, QUARTERS)
         px(c, q).wait_recv()
+        if g < rounds:
+            tell_near(far.at[g])
 
         @pl.when(has_to)
         def _():
@@ -226,8 +242,10 @@
             for t in range(1, chips):
                 ay(t, c, h).wait_recv()
                 af(t, c, h).start()
-        if g >= LAG:
+        if 0 <= g - LAG:
             finish(g - LAG)
+        if g < rounds:
+            pl.semaphore_wait(far.at[g], near)
     for g in range(total - LAG, total):
         finish(g)
 
@@ -295,6 +313,7 @@
     rows = planes * cells // LANES
     scale = 1.0 / (8.0 * math.sqrt(comps * planes * slabs * cells))
     reduce_here = cols % (8 * slabs) == 0
+    rounds = slabs // 2 - 1 if reduce_here else 0
     share = cols // slabs if reduce_here else 8
     halves = (snaps // 2, comps, HALVES)
     quarters = (comps, QUARTERS)
@@ -305,20 +324,24 @@
     out = pl.pallas_call(
         functools.partial(kernel, slabs, snaps, reduce_here, scale),
         out_shape=jax.ShapeDtypeStruct((cols, snaps * cols), jnp.float32),
-        in_specs=[hbm, hbm, vmem, vmem, vmem],
+        in_specs=[hbm] * 5,
         out_specs=vmem,
         scratch_shapes=[
+            pltpu.VMEM((rows, LANES), jnp.float32),
+            pltpu.VMEM((cells // LANES, LANES), jnp.float32),
+            pltpu.VMEM((LANES, 3 * LANES), jnp.bfloat16),
+            pltpu.SemaphoreType.REGULAR((max(rounds, 1),)),
             pltpu.VMEM(block, jnp.bfloat16),
             pltpu.VMEM((2,) + block, jnp.bfloat16),
             pltpu.VMEM((snaps,) + block, jnp.bfloat16),
-            pltpu.VMEM((snaps * cols * rows, LANES), jnp.float32),
+            pltpu.VMEM((cols // HALVES * rows, LANES), jnp.float32),
             pltpu.VMEM((cols * rows, LANES), jnp.float32),
             pltpu.VMEM((snaps * cols, rows * LANES), jnp.bfloat16),
             pltpu.VMEM((cols, rows * LANES), jnp.bfloat16),
             pltpu.VMEM((rows, LANES), jnp.float32),
             pltpu.VMEM((cols, snaps * cols), jnp.float32),
             pltpu.VMEM((max(slabs, 1) if reduce_here else 1, share, snaps * cols), jnp.float32),
-            dma((2, comps)),
+            dma((3, max(comps, 3))),
             dma(quarters), dma(quarters),
             dma(quarters), dma(quarters),
             dma((comps,)), dma((comps,)),

time: 44.5 us -> 40.3 us (0.906)
  Pallas kernels: 42.8 us -> 38.6 us
    pallas_call x1, Pallas kernels: 42.8 us -> 38.6 us  [per_device(): pl.pallas_call(functools.partial(kernel, slabs, snaps, reduce_here, scale...]
where the time goes in v2:
time: 40.3 us; the launch traced here: 40.1 us
  Pallas kernels  38.6 us (96%)
  local copies, waits for them, and re-layouts  1.47 us (4%)
    pallas_call x1, Pallas kernels, per_device(): pl.pallas_call(functools.partial(kernel, slabs, snaps, reduce_here, scale...  38.6 us
    unnamed x1, local copies, waits for them, and re-layouts  1.47 us

profile of v2, /device:TPU:0, one launch (start us, length us, event | category | flops | bytes accessed | tf_op | source)
XLA Modules:
  0.0 40.1 jit_solution(11500395040999210949)
XLA Ops:
  0.0 38.6 %shard_map.55 = f32[64,256]{1,0:T(8,128)} custom-call(bf16[64,3,16,128]{3,2,1,0:T(8,128)(2,1)} %bitcast.17, bf16[64,3,16,128]{3,2,1,0:T(8,128)(2,1)} %bitcast.18, f32[16,128]{1,0:T(8,128)} %bitcast.20, f32[8,128]{1,0:T(8,128)} %bitcast.21, bf16[128,384]{1,0:T(8,128)(2,1)} %constant.2.clone.m_hbm), custom_call_target="tpu_custom_call" | custom-call | tf_op jit(solution)/shard_map/pallas_call | solution.py:324
  38.6 1.5 %copy.10 = f32[256,64]{0,1:T(8,128)} copy(f32[256,64]{0,1:T(8,128)} %bitcast.19) | data formatting | bytes 131072

commit v3 on v2

--- a/solution.py
+++ b/solution.py
@@ -14,7 +14,7 @@
 LANES = 128
 QUARTERS = 4
 HALVES = 2
-LAG = 2
+LAG = 3
 GROUP = 16
 
 
@@ -278,14 +278,19 @@
         rs[0] = summed
         for k in range(1, slabs):
             gather(k).start()
-        out_ref[rows_of(i), :] = summed
+        own = pltpu.make_async_copy(rs.at[0], out_ref.at[rows_of(i)], loc_sem.at[0, 0])
+        own.start()
         for k in range(1, slabs):
             gathered(k).wait_recv()
+        own.wait()
         for k in range(1, slabs):
             scatter(k).wait_send()
             gather(k).wait_send()
     else:
-        out_ref[...] = acc[...] * scale
+        acc[...] = acc[...] * scale
+        whole = pltpu.make_async_copy(acc, out_ref, loc_sem.at[0, 0])
+        whole.start()
+        whole.wait()
 
     for c in range(comps):
         ac(c).wait_send()
@@ -319,13 +324,12 @@
     quarters = (comps, QUARTERS)
     dma = pltpu.SemaphoreType.DMA
     block = (cols, comps, rows, LANES)
-    vmem = pl.BlockSpec(memory_space=pltpu.VMEM)
     hbm = pl.BlockSpec(memory_space=pltpu.HBM)
     out = pl.pallas_call(
         functools.partial(kernel, slabs, snaps, reduce_here, scale),
         out_shape=jax.ShapeDtypeStruct((cols, snaps * cols), jnp.float32),
         in_specs=[hbm] * 5,
-        out_specs=vmem,
+        out_specs=hbm,
         scratch_shapes=[
             pltpu.VMEM((rows, LANES), jnp.float32),
             pltpu.VMEM((cells // LANES, LANES), jnp.float32),

time: 40.3 us -> 38.3 us (0.950)
  Pallas kernels: 38.6 us -> 36.7 us
    pallas_call x1, Pallas kernels: 38.6 us -> 36.7 us  [per_device(): pl.pallas_call(functools.partial(kernel, slabs, snaps, reduce_here, scale...]
where the time goes in v3:
time: 38.3 us; the launch traced here: 38.1 us
  Pallas kernels  36.7 us (96%)
  local copies, waits for them, and re-layouts  1.47 us (4%)
    pallas_call x1, Pallas kernels, per_device(): pl.pallas_call(functools.partial(kernel, slabs, snaps, reduce_here, scale...  36.7 us
    unnamed x1, local copies, waits for them, and re-layouts  1.47 us

profile of v3, /device:TPU:0, one launch (start us, length us, event | category | flops | bytes accessed | tf_op | source)
XLA Modules:
  0.0 38.1 jit_solution(6488481418072040419)
XLA Ops:
  0.0 36.7 %shard_map.55 = f32[64,256]{1,0:T(8,128)} custom-call(bf16[64,3,16,128]{3,2,1,0:T(8,128)(2,1)} %bitcast.17, bf16[64,3,16,128]{3,2,1,0:T(8,128)(2,1)} %bitcast.18, f32[16,128]{1,0:T(8,128)} %bitcast.20, f32[8,128]{1,0:T(8,128)} %bitcast.21, bf16[128,384]{1,0:T(8,128)(2,1)} %constant.2.clone.m_hbm), custom_call_target="tpu_custom_call" | custom-call | tf_op jit(solution)/shard_map/pallas_call | solution.py:328
  36.7 1.5 %copy.10 = f32[256,64]{0,1:T(8,128)} copy(f32[256,64]{0,1:T(8,128)} %bitcast.19) | data formatting | bytes 131072

commit v4 on v3

--- a/solution.py
+++ b/solution.py
@@ -14,7 +14,7 @@
 LANES = 128
 QUARTERS = 4
 HALVES = 2
-LAG = 3
+LAG = 4
 GROUP = 16
 
 

time: 38.3 us -> 38.1 us (level)
  no operation moved by 1% of the time
where the time goes in v4:
time: 38.1 us; the launch traced here: 38 us
  Pallas kernels  36.5 us (96%)
  local copies, waits for them, and re-layouts  1.47 us (4%)
    pallas_call x1, Pallas kernels, per_device(): pl.pallas_call(functools.partial(kernel, slabs, snaps, reduce_here, scale...  36.5 us
    unnamed x1, local copies, waits for them, and re-layouts  1.47 us

profile of v4, /device:TPU:0, one launch (start us, length us, event | category | flops | bytes accessed | tf_op | source)
XLA Modules:
  0.0 38.0 jit_solution(4157003046861263768)
XLA Ops:
  0.0 36.5 %shard_map.55 = f32[64,256]{1,0:T(8,128)} custom-call(bf16[64,3,16,128]{3,2,1,0:T(8,128)(2,1)} %bitcast.17, bf16[64,3,16,128]{3,2,1,0:T(8,128)(2,1)} %bitcast.18, f32[16,128]{1,0:T(8,128)} %bitcast.20, f32[8,128]{1,0:T(8,128)} %bitcast.21, bf16[128,384]{1,0:T(8,128)(2,1)} %constant.2.clone.m_hbm), custom_call_target="tpu_custom_call" | custom-call | tf_op jit(solution)/shard_map/pallas_call | solution.py:328
  36.5 1.5 %copy.10 = f32[256,64]{0,1:T(8,128)} copy(f32[256,64]{0,1:T(8,128)} %bitcast.19) | data formatting | bytes 131072
